TPU v7x, 32 devices: a whole 2x2x4 slice. The times are simulated.
32 devices in a mesh: regions: 2 (over y), gz: 8 (over z, x), gy: 2 (over core).
Axes of the slice: x: 2, y: 2, z: 4, core: 2. Of those that a mesh axis runs over, the one named last changes fastest.
Arguments:
- iterate: float32 [16, 32, 128, 256], P(None, ('regions', 'gz'), 'gy'), parts along dimension 1, may hold values from -6 to 6
- residual: float32 [16, 32, 128, 256], P(None, ('regions', 'gz'), 'gy'), parts along dimension 1, may hold values from -16 to 16
- labels: int32 [32, 128, 256], P(('regions', 'gz'), 'gy'), parts along dimension 0, may hold values from 0 to 7
- boundary: int32 [32, 128, 256], P(('regions', 'gz'), 'gy'), parts along dimension 0, may hold values 0 or 1
Outputs:
- iterate_out: float32 [16, 32, 128, 256], P(None, ('regions', 'gz'), 'gy'), parts along dimension 1
- residual_out: float32 [16, 32, 128, 256], P(None, ('regions', 'gz'), 'gy'), parts along dimension 1
There are 2 independent parts, one for each index of `regions`. A program takes and returns all parts, laid end to end along the dimension named above; each array names one. Nothing has to cross between parts.
All inputs are finite; a program needn't handle non-finite values. No bound on the sum of `boundary` on one device may be relied on, other than what follows from the above.
Results may differ from a plain program's by a relative error of at most 0.0003.
Values sent between devices are 32-bit elements; how exact they have to be, the bound alone decides.
A program may use at most 128 MiB of HBM per device.

v0:
```python
import math
import jax
import jax.numpy as jnp
from jax import lax
from jax.sharding import PartitionSpec as P

NCLASS = 8
ITERS = 3
contrast_log = 4.0 * math.log(10.0)
highest = lax.Precision.HIGHEST


def extended_2(cells, sides, width):
    for axis, dim in sides:
        count = lax.axis_size(axis)
        ends = count - 1
        head = lax.slice_in_dim(cells, 0, width, axis=dim)
        tail = lax.slice_in_dim(cells, cells.shape[dim] - width, cells.shape[dim], axis=dim)
        cells = jnp.concatenate(
            [
                lax.ppermute(tail, axis, [(i, (i + 1) % count) for i in range(ends)]),
                cells,
                lax.ppermute(head, axis, [((i + 1) % count, i) for i in range(ends)]),
            ],
            axis=dim,
        )
    return cells


def shift_cells(block, forward):
    widths = [(0, 0)] * (block.ndim - 1)
    if forward:
        return jnp.pad(block[..., 1:], widths + [(0, 1)])
    return jnp.pad(block[..., :-1], widths + [(1, 0)])


def neighbors(extended):
    center = extended[..., 1:-1, 1:-1, :]
    beside = [
        extended[..., 2:, 1:-1, :],
        extended[..., :-2, 1:-1, :],
        extended[..., 1:-1, 2:, :],
        extended[..., 1:-1, :-2, :],
        shift_cells(center, True),
        shift_cells(center, False),
    ]
    return (center, beside)


def couplings_of(extended):
    coef_center, coef_beside = neighbors(extended[0])
    inner_center, inner_beside = neighbors(extended[1])
    diagonal = jnp.zeros_like(coef_center)
    offsets = []
    for neighbor_coef, neighbor_inner in zip(coef_beside, inner_beside):
        face_coef = jnp.where(
            neighbor_coef > 0.0,
            2.0 * coef_center * neighbor_coef / (coef_center + neighbor_coef),
            coef_center,
        )
        diagonal = diagonal + face_coef
        offsets.append(inner_center * face_coef * neighbor_inner)
    diagonal = inner_center * diagonal + (1.0 - inner_center)
    return (diagonal, offsets)


def apply_operator(diagonal, offsets, extended):
    center, beside = neighbors(extended)
    coupled = offsets[0] * beside[0]
    for weight, values in zip(offsets[1:], beside[1:]):
        coupled = coupled + weight * values
    return diagonal * center - coupled


def cell_fields(labels, boundary):
    coef = jnp.exp(labels.astype(jnp.float32) * (contrast_log / (NCLASS - 1)))
    interior = (1 - boundary).astype(jnp.float32)
    return jnp.stack([coef, interior])


def gram(left_block, right_block):
    left_flat = left_block.reshape(left_block.shape[0], -1)
    right_flat = right_block.reshape(right_block.shape[0], -1)
    return lax.dot_general(left_flat, right_flat, (((1,), (1,)), ((), ())), precision=highest)


def combine(block, weights):
    flat = block.reshape(block.shape[0], -1)
    mixed = lax.dot_general(weights, flat, (((0,), (0,)), ((), ())), precision=highest)
    return mixed.reshape(block.shape)


def spd_solve(matrix, right):
    factor = jnp.linalg.cholesky(matrix)
    return jax.scipy.linalg.cho_solve((factor, True), right)


def direction_cells(field):
    return extended_2(field, (("gz", 1), ("gy", 2)), 1)


def on_device(iterate, residual, labels, boundary):
    fields = cell_fields(labels, boundary)
    extended = extended_2(fields, (("gz", 1), ("gy", 2)), 1)
    diagonal, offsets = couplings_of(extended)
    inverse_diag = 1.0 / diagonal
    scaled = inverse_diag * residual
    direction = scaled
    for iteration in range(ITERS):
        direction_ext = direction_cells(direction)
        image = apply_operator(diagonal, offsets, direction_ext)
        weighted = inverse_diag * image
        summed_rho, curvature, cross_gram, image_gram = lax.psum(
            (
                gram(residual, scaled),
                gram(direction, image),
                gram(scaled, image),
                gram(image, weighted),
            ),
            ("gz", "gy"),
        )
        step_size = spd_solve(curvature, summed_rho)
        iterate = iterate + combine(direction, step_size)
        residual = residual - combine(image, step_size)
        if iteration + 1 < ITERS:
            scaled = inverse_diag * residual
            moved = jnp.dot(cross_gram, step_size, precision=highest)
            quadratic = jnp.dot(
                step_size.T, jnp.dot(image_gram, step_size, precision=highest), precision=highest
            )
            next_rho = summed_rho - moved - moved.T + quadratic
            momentum = spd_solve(summed_rho, next_rho)
            direction = scaled + combine(direction, momentum)
            summed_rho = next_rho
    return (iterate, residual)


def solution(mesh):
    placed = (
        P(None, ("regions", "gz"), "gy", None),
        P(None, ("regions", "gz"), "gy", None),
        P(("regions", "gz"), "gy", None),
        P(("regions", "gz"), "gy", None),
    )
    return jax.shard_map(
        on_device,
        mesh=mesh,
        in_specs=placed,
        out_specs=(P(None, ("regions", "gz"), "gy", None), P(None, ("regions", "gz"), "gy", None)),
        check_vma=False,
    )
```

profile of v0, /device:TPU:0, one launch (start us, length us, event | category | flops | bytes accessed | tf_op | source)
XLA Modules:
  0.0 462.8 jit_solution(4175048000201397154)
XLA Ops:
  2.5 1.3 collective-permute-start.1
  3.8 5.5 %collective-permute-start = (f32[2,1,64,256]{3,2,1,0:T(8,128)S(1)}, f32[2,1,64,256]{3,2,1,0:T(8,128)S(1)}, u32[]{:S(2)}, u32[]{:S(2)}) collective-permute-start(f32[2,1,64,256]{3,2,1,0:T(8,128)S(1)} %get-tuple-element.51), channel_id=1, source_target_pairs={{0,2},{2,4},{4,6},{6,8},{8,10},{10,12},{12,14},{1,3},{3,5},{5,7},{... | collective-permute-start | bytes 393224 | tf_op jit(solution)/shard_map/ppermute | solution.py:21
  9.3 1.5 collective-permute-done.1
  10.9 3.0 collective-permute-done
  13.9 1.3 collective-permute-start.3
  15.2 3.0 collective-permute-start.2
  22.1 1.3 collective-permute-start.4
  23.4 5.1 %collective-permute-start.5 = (f32[16,1,64,256]{3,0,2,1:T(8,128)S(1)}, f32[16,1,64,256]{3,0,2,1:T(8,128)S(1)}, u32[]{:S(2)}, u32[]{:S(2)}) collective-permute-start(f32[16,1,64,256]{3,0,2,1:T(8,128)S(1)} %get-tuple-element.35), channel_id=1, source_target_pairs={{0,2},{2,4},{4,6},{6,8},{8,10},{10,12},{12,14},{1,3},{3,5},{5,7},{... | collective-permute-start | bytes 3145736 | tf_op jit(solution)/shard_map/ppermute | solution.py:21
  28.5 3.5 fusion.74
  32.7 17.4 %collective-permute-done.4 = f32[16,1,64,256]{3,0,2,1:T(8,128)S(1)} collective-permute-done((f32[16,1,64,256]{3,0,2,1:T(8,128)S(1)}, f32[16,1,64,256]{3,0,2,1:T(8,128)S(1)}, u32[]{:S(2)}, u32[]{:S(2)}) %collective-permute-start.4) | collective-permute-done | bytes 1048608 | tf_op jit(solution)/shard_map/ppermute | solution.py:23
  50.1 22.6 %collective-permute-done.5 = f32[16,1,64,256]{3,0,2,1:T(8,128)S(1)} collective-permute-done((f32[16,1,64,256]{3,0,2,1:T(8,128)S(1)}, f32[16,1,64,256]{3,0,2,1:T(8,128)S(1)}, u32[]{:S(2)}, u32[]{:S(2)}) %collective-permute-start.5) | collective-permute-done | bytes 1048608 | tf_op jit(solution)/shard_map/ppermute | solution.py:21
  72.8 1.9 collective-permute-start.7
  74.7 1.5 collective-permute-start.6
  76.4 2.5 copy.93
  79.0 3.2 fusion.34
  82.2 3.8 convolution_bitcast_fusion.5
  86.0 2.7 fusion.86
  88.8 2.6 copy.95
  91.3 60.9 %all-reduce.12 = (f32[16,16]{0,1:T(8,128)S(1)}, f32[16,16]{0,1:T(8,128)S(1)}, f32[16,16]{1,0:T(8,128)S(1)}) all-reduce(f32[16,16]{0,1:T(8,128)S(1)} %fusion.74, f32[16,16]{0,1:T(8,128)S(1)} %convolution_bitcast_fusion.5, f32[16,16]{1,0:T(8,128)S(1)} %fusion.86), channel_id=1, replica_groups=mesh['regions'=2,'gz'=8,'gy'=2] {'gz','gy'}, use_global_device_ids=true, to_apply=%region_3.5 | all-reduce | flops 768 | bytes 6144 | tf_op jit(solution)/shard_map/psum | solution.py:113
  152.3 1.5 cholesky.89
  155.2 1.2 custom-call.11
  157.0 6.3 %copy_subtract_fusion = f32[16,2,64,256]{3,0,2,1:T(8,128)S(1)} fusion(f32[16,2,64,256]{3,2,1,0:T(8,128)} %param.8, f32[2,64,256,16]{2,1,0,3:T(8,128)} %bitcast.241, f32[16,16]{1,0:T(8,128)S(1)} %fusion.124), kind=kOutput, calls=%fused_computation.85 | convolution fusion | flops 101187584 | bytes 6292480 | tf_op jit(solution)/shard_map/dot_general | solution.py:89
  163.5 1.5 cholesky.100
  166.3 1.2 custom-call.12
  168.1 4.5 multiply_add_fusion.1
  172.8 1.3 collective-permute-start.8
  174.1 4.6 collective-permute-start.9
  179.5 15.8 %collective-permute-done.8 = f32[16,1,64,256]{3,0,2,1:T(8,128)S(1)} collective-permute-done((f32[16,1,64,256]{3,0,2,1:T(8,128)S(1)}, f32[16,1,64,256]{3,0,2,1:T(8,128)S(1)}, u32[]{:S(2)}, u32[]{:S(2)}) %collective-permute-start.8) | collective-permute-done | bytes 1048608 | tf_op jit(solution)/shard_map/ppermute | solution.py:23
  195.3 18.0 %collective-permute-done.9 = f32[16,1,64,256]{3,0,2,1:T(8,128)S(1)} collective-permute-done((f32[16,1,64,256]{3,0,2,1:T(8,128)S(1)}, f32[16,1,64,256]{3,0,2,1:T(8,128)S(1)}, u32[]{:S(2)}, u32[]{:S(2)}) %collective-permute-start.9) | collective-permute-done | bytes 1048608 | tf_op jit(solution)/shard_map/ppermute | solution.py:21
  213.2 1.9 collective-permute-start.11
  215.2 1.8 collective-permute-start.10
  216.9 2.8 fusion.77
  219.7 2.6 copy.97
  222.3 3.2 fusion.24
  225.5 2.9 convolution_bitcast_fusion.3
  228.4 2.8 fusion.89
  231.2 2.8 fusion.80
  234.0 2.6 copy.99
  236.6 62.6 %all-reduce.11 = (f32[16,16]{0,1:T(8,128)S(1)}, f32[16,16]{0,1:T(8,128)S(1)}, f32[16,16]{1,0:T(8,128)S(1)}, f32[16,16]{1,0:T(8,128)S(1)}) all-reduce(f32[16,16]{0,1:T(8,128)S(1)} %fusion.77, f32[16,16]{0,1:T(8,128)S(1)} %convolution_bitcast_fusion.3, f32[16,16]{1,0:T(8,128)S(1)} %fusion.89, ...), channel_id=1, replica_groups=mesh['regions'=2,'gz'=8,'gy'=2] {'gz','gy'}, use_global_device_ids=true, to_apply=%region_6.9 | all-reduce | flops 1024 | bytes 8192 | tf_op jit(solution)/shard_map/psum | solution.py:113
  299.2 1.5 cholesky.111
  301.9 1.2 custom-call.13
  303.5 5.7 %fusion.68 = f32[16,2,64,256]{3,0,2,1:T(8,128)} fusion(f32[16,2,64,256]{3,0,2,1:T(8,128)S(1)} %copy_subtract_fusion, f32[2,64,256,16]{2,1,0,3:T(8,128)} %bitcast.240, f32[16,16]{1,0:T(8,128)S(1)} %fusion.113), kind=kOutput, calls=%fused_computation.89 | convolution fusion | flops 101187584 | bytes 6292480 | tf_op jit(solution)/shard_map/dot_general | solution.py:89
  309.5 1.5 cholesky.122
  312.3 1.2 custom-call.14
  314.1 5.2 %multiply_add_fusion = f32[16,2,64,256]{3,0,2,1:T(8,128)S(1)} fusion(f32[16,2,64,256]{3,0,2,1:T(8,128)} %fusion.68, f32[16,16,1,1]{0,1,3,2:T(8,128)S(1)} %convolution_bitcast_fusion.2, f32[2,64,256,16]{2,1,0,3:T(8,128)} %bitcast.234, f32[2,64,256]{2,1,0:T(8,128)S(1)} %get-tuple-element.17), kind=kOutput, calls=%fused_computation.6 | convolution fusion | flops 101711872 | bytes 6423552 | tf_op jit(solution)/shard_map/dot_general | solution.py:89
  319.5 1.4 collective-permute-start.12
  320.9 4.6 collective-permute-start.13
  325.6 4.2 fusion.52
  330.5 11.6 %collective-permute-done.12 = f32[16,1,64,256]{3,0,2,1:T(8,128)S(1)} collective-permute-done((f32[16,1,64,256]{3,0,2,1:T(8,128)S(1)}, f32[16,1,64,256]{3,0,2,1:T(8,128)S(1)}, u32[]{:S(2)}, u32[]{:S(2)}) %collective-permute-start.12) | collective-permute-done | bytes 1048608 | tf_op jit(solution)/shard_map/ppermute | solution.py:23
  342.1 18.0 %collective-permute-done.13 = f32[16,1,64,256]{3,0,2,1:T(8,128)S(1)} collective-permute-done((f32[16,1,64,256]{3,0,2,1:T(8,128)S(1)}, f32[16,1,64,256]{3,0,2,1:T(8,128)S(1)}, u32[]{:S(2)}, u32[]{:S(2)}) %collective-permute-start.13) | collective-permute-done | bytes 1048608 | tf_op jit(solution)/shard_map/ppermute | solution.py:21
  360.0 1.9 collective-permute-start.15
  362.0 1.3 collective-permute-start.14
  363.3 2.7 fusion.83
  366.0 2.6 copy.101
  368.6 3.2 fusion.14
  371.8 1.3 copy-done.4
  373.1 2.9 convolution_bitcast_fusion.1
  376.0 62.5 %all-reduce.10 = (f32[16,16]{1,0:T(8,128)S(1)}, f32[16,16]{0,1:T(8,128)S(1)}) all-reduce(f32[16,16]{1,0:T(8,128)S(1)} %fusion.83, f32[16,16]{0,1:T(8,128)S(1)} %convolution_bitcast_fusion.1), channel_id=1, replica_groups=mesh['regions'=2,'gz'=8,'gy'=2] {'gz','gy'}, use_global_device_ids=true, to_apply=%region_10.13 | all-reduce | flops 512 | bytes 4096 | tf_op jit(solution)/shard_map/psum | solution.py:113
  438.6 1.5 cholesky.133
  442.9 4.5 fusion.42
  447.5 5.7 %fusion.49 = f32[16,2,64,256]{3,0,2,1:T(8,128)S(1)} fusion(f32[16,2,64,256]{3,0,2,1:T(8,128)S(1)} %fusion.42, f32[16,2,64,256]{3,0,2,1:T(8,128)S(1)} %copy-done.6, f32[16,2,64,256]{3,2,1,0:T(8,128)} %param.7, f32[2,64,256,16]{2,1,0,3:T(8,128)S(1)} %bitcast.237, f32[16,16]{1,0:T(8,128)S(1)} %fusion.124), kind=kOutput, calls=%fused_computation.76 | convolution fusion | flops 102236160 | bytes 10486784 | tf_op jit(solution)/shard_map/dot_general | solution.py:89
  453.2 2.5 copy.64
  457.0 2.9 fusion.71
  459.8 2.5 copy.65
  (85 shorter events, 20.9 us)
Async XLA Ops:
  2.5 8.4 %collective-permute-start.1 = (f32[2,1,64,256]{3,2,1,0:T(8,128)S(1)}, f32[2,1,64,256]{3,2,1,0:T(8,128)S(1)}, u32[]{:S(2)}, u32[]{:S(2)}) collective-permute-start(f32[2,1,64,256]{3,2,1,0:T(8,128)S(1)} %get-tuple-element.52), channel_id=1, source_target_pairs={{2,0},{4,2},{6,4},{8,6},{10,8},{12,10},{14,12},{3,1},{5,3},{7,5},{... | collective-permute-start | bytes 393224 | tf_op jit(solution)/shard_map/ppermute | solution.py:23
  3.8 10.0 %collective-permute-start = (f32[2,1,64,256]{3,2,1,0:T(8,128)S(1)}, f32[2,1,64,256]{3,2,1,0:T(8,128)S(1)}, u32[]{:S(2)}, u32[]{:S(2)}) collective-permute-start(f32[2,1,64,256]{3,2,1,0:T(8,128)S(1)} %get-tuple-element.51), channel_id=1, source_target_pairs={{0,2},{2,4},{4,6},{6,8},{8,10},{10,12},{12,14},{1,3},{3,5},{5,7},{... | collective-permute-start | bytes 393224 | tf_op jit(solution)/shard_map/ppermute | solution.py:21
  13.9 4.3 collective-permute-start.3
  15.2 3.8 collective-permute-start.2
  19.1 1.6 copy-start
  22.1 28.1 %collective-permute-start.4 = (f32[16,1,64,256]{3,0,2,1:T(8,128)S(1)}, f32[16,1,64,256]{3,0,2,1:T(8,128)S(1)}, u32[]{:S(2)}, u32[]{:S(2)}) collective-permute-start(f32[16,1,64,256]{3,0,2,1:T(8,128)S(1)} %get-tuple-element.36), channel_id=1, source_target_pairs={{2,0},{4,2},{6,4},{8,6},{10,8},{12,10},{14,12},{3,1},{5,3},{7,5},{... | collective-permute-start | bytes 3145736 | tf_op jit(solution)/shard_map/ppermute | solution.py:23
  23.4 49.4 %collective-permute-start.5 = (f32[16,1,64,256]{3,0,2,1:T(8,128)S(1)}, f32[16,1,64,256]{3,0,2,1:T(8,128)S(1)}, u32[]{:S(2)}, u32[]{:S(2)}) collective-permute-start(f32[16,1,64,256]{3,0,2,1:T(8,128)S(1)} %get-tuple-element.35), channel_id=1, source_target_pairs={{0,2},{2,4},{4,6},{6,8},{8,10},{10,12},{12,14},{1,3},{3,5},{5,7},{... | collective-permute-start | bytes 3145736 | tf_op jit(solution)/shard_map/ppermute | solution.py:21
  72.8 6.2 %collective-permute-start.7 = (f32[16,4,1,256]{3,0,2,1:T(8,128)S(1)}, f32[16,4,1,256]{3,0,2,1:T(8,128)S(1)}, u32[]{:S(2)}, u32[]{:S(2)}) collective-permute-start(f32[16,4,1,256]{3,0,2,1:T(8,128)S(1)} %get-tuple-element.24), channel_id=1, source_target_pairs={{0,1},{2,3},{4,5},{6,7},{8,9},{10,11},{12,13},{14,15},{16,17},{18,... | collective-permute-start | bytes 196616 | tf_op jit(solution)/shard_map/ppermute | solution.py:21
  74.7 4.3 collective-permute-start.6
  172.8 22.4 %collective-permute-start.8 = (f32[16,1,64,256]{3,0,2,1:T(8,128)S(1)}, f32[16,1,64,256]{3,0,2,1:T(8,128)S(1)}, u32[]{:S(2)}, u32[]{:S(2)}) collective-permute-start(f32[16,1,64,256]{3,0,2,1:T(8,128)S(1)} %get-tuple-element.32), channel_id=1, source_target_pairs={{2,0},{4,2},{6,4},{8,6},{10,8},{12,10},{14,12},{3,1},{5,3},{7,5},{... | collective-permute-start | bytes 3145736 | tf_op jit(solution)/shard_map/ppermute | solution.py:23
  174.1 39.1 %collective-permute-start.9 = (f32[16,1,64,256]{3,0,2,1:T(8,128)S(1)}, f32[16,1,64,256]{3,0,2,1:T(8,128)S(1)}, u32[]{:S(2)}, u32[]{:S(2)}) collective-permute-start(f32[16,1,64,256]{3,0,2,1:T(8,128)S(1)} %get-tuple-element.31), channel_id=1, source_target_pairs={{0,2},{2,4},{4,6},{6,8},{8,10},{10,12},{12,14},{1,3},{3,5},{5,7},{... | collective-permute-start | bytes 3145736 | tf_op jit(solution)/shard_map/ppermute | solution.py:21
  213.2 9.0 %collective-permute-start.11 = (f32[16,4,1,256]{3,0,2,1:T(8,128)S(1)}, f32[16,4,1,256]{3,0,2,1:T(8,128)S(1)}, u32[]{:S(2)}, u32[]{:S(2)}) collective-permute-start(f32[16,4,1,256]{3,0,2,1:T(8,128)S(1)} %get-tuple-element.22), channel_id=1, source_target_pairs={{0,1},{2,3},{4,5},{6,7},{8,9},{10,11},{12,13},{14,15},{16,17},{18,... | collective-permute-start | bytes 196616 | tf_op jit(solution)/shard_map/ppermute | solution.py:21
  215.2 7.1 %collective-permute-start.10 = (f32[16,4,1,256]{3,0,2,1:T(8,128)S(1)}, f32[16,4,1,256]{3,0,2,1:T(8,128)S(1)}, u32[]{:S(2)}, u32[]{:S(2)}) collective-permute-start(f32[16,4,1,256]{3,0,2,1:T(8,128)S(1)} %get-tuple-element.21), channel_id=1, source_target_pairs={{1,0},{3,2},{5,4},{7,6},{9,8},{11,10},{13,12},{15,14},{17,16},{19,... | collective-permute-start | bytes 196616 | tf_op jit(solution)/shard_map/ppermute | solution.py:23
  319.3 6.2 %copy-start.2 = (f32[2,8,128,256]{3,2,1,0:T(8,128)S(1)}, f32[2,8,128,256]{3,2,1,0:T(8,128)}, u32[]{:S(2)}) copy-start(f32[2,8,128,256]{3,2,1,0:T(8,128)} %copy.97) | copy-start | bytes 6291460
  319.5 22.6 %collective-permute-start.12 = (f32[16,1,64,256]{3,0,2,1:T(8,128)S(1)}, f32[16,1,64,256]{3,0,2,1:T(8,128)S(1)}, u32[]{:S(2)}, u32[]{:S(2)}) collective-permute-start(f32[16,1,64,256]{3,0,2,1:T(8,128)S(1)} %get-tuple-element.28), channel_id=1, source_target_pairs={{2,0},{4,2},{6,4},{8,6},{10,8},{12,10},{14,12},{3,1},{5,3},{7,5},{... | collective-permute-start | bytes 3145736 | tf_op jit(solution)/shard_map/ppermute | solution.py:23
  320.9 39.1 %collective-permute-start.13 = (f32[16,1,64,256]{3,0,2,1:T(8,128)S(1)}, f32[16,1,64,256]{3,0,2,1:T(8,128)S(1)}, u32[]{:S(2)}, u32[]{:S(2)}) collective-permute-start(f32[16,1,64,256]{3,0,2,1:T(8,128)S(1)} %get-tuple-element.27), channel_id=1, source_target_pairs={{0,2},{2,4},{4,6},{6,8},{8,10},{10,12},{12,14},{1,3},{3,5},{5,7},{... | collective-permute-start | bytes 3145736 | tf_op jit(solution)/shard_map/ppermute | solution.py:21
  330.5 32.8 %copy-start.1 = (f32[16,2,64,256]{3,0,2,1:T(8,128)S(1)}, f32[16,2,64,256]{3,0,2,1:T(8,128)}, u32[]{:S(2)}) copy-start(f32[16,2,64,256]{3,0,2,1:T(8,128)} %fusion.68) | copy-start | bytes 6291460
  360.0 8.5 %collective-permute-start.15 = (f32[16,4,1,256]{3,0,2,1:T(8,128)S(1)}, f32[16,4,1,256]{3,0,2,1:T(8,128)S(1)}, u32[]{:S(2)}, u32[]{:S(2)}) collective-permute-start(f32[16,4,1,256]{3,0,2,1:T(8,128)S(1)} %get-tuple-element.20), channel_id=1, source_target_pairs={{0,1},{2,3},{4,5},{6,7},{8,9},{10,11},{12,13},{14,15},{16,17},{18,... | collective-permute-start | bytes 196616 | tf_op jit(solution)/shard_map/ppermute | solution.py:21
  362.0 6.6 %collective-permute-start.14 = (f32[16,4,1,256]{3,0,2,1:T(8,128)S(1)}, f32[16,4,1,256]{3,0,2,1:T(8,128)S(1)}, u32[]{:S(2)}, u32[]{:S(2)}) collective-permute-start(f32[16,4,1,256]{3,0,2,1:T(8,128)S(1)} %get-tuple-element.19), channel_id=1, source_target_pairs={{1,0},{3,2},{5,4},{7,6},{9,8},{11,10},{13,12},{15,14},{17,16},{19,... | collective-permute-start | bytes 196616 | tf_op jit(solution)/shard_map/ppermute | solution.py:23
  371.8 1.3 copy-start.4
  442.9 4.6 copy-start.3
  442.9 4.6 copy-start.6
  453.2 2.5 copy-start.5
where the time goes:
time: 469 us; the launch traced here: 463 us
  blocking collectives  186 us (40%)
  waiting for transfers between devices  109 us (23%)
  matrix products  68.6 us (15%)
  starting transfers between devices  39.8 us (8%)
  other arithmetic  33.3 us (7%)
  local copies, waits for them, and re-layouts  24.9 us (5%)
    psum x3, blocking collectives, on_device(): lax.psum((gram(residual, scaled), gram(direction, image), gram(scaled, im...  186 us
    ppermute x8, waiting for transfers between devices, extended_2(): lax.ppermute(tail, axis, [(i, (i + 1) % count) for i in range(ends)])  62.3 us
    ppermute x8, waiting for transfers between devices, extended_2(): lax.ppermute(head, axis, [((i + 1) % count, i) for i in range(ends)])  46.3 us
    dot_general x8, matrix products, combine(): lax.dot_general(weights, flat, (((0,), (0,)), ((), ())), precision=highest)  38.9 us
    ppermute x8, starting transfers between devices, extended_2(): lax.ppermute(tail, axis, [(i, (i + 1) % count) for i in range(ends)])  28.6 us
    dot_general x9, matrix products, gram(): lax.dot_general(left_flat, right_flat, (((1,), (1,)), ((), ())), precisio...  26.8 us
    unnamed x22, local copies, waits for them, and re-layouts  21.5 us
    ppermute x8, starting transfers between devices, extended_2(): lax.ppermute(head, axis, [((i + 1) % count, i) for i in range(ends)])  11.1 us
  transfers between devices with their start and end apart: 16, of which 9 were waited for; matrix products, arithmetic and copies ran while one was open for 5% of the time, Pallas kernels for 0%

commit v1 on v0

--- a/solution.py
+++ b/solution.py
@@ -111,13 +111,16 @@
         image = apply_operator(diagonal, offsets, direction_ext)
         weighted = inverse_diag * image
         summed_rho, curvature, cross_gram, image_gram = lax.psum(
-            (
-                gram(residual, scaled),
-                gram(direction, image),
-                gram(scaled, image),
-                gram(image, weighted),
+            lax.psum(
+                (
+                    gram(residual, scaled),
+                    gram(direction, image),
+                    gram(scaled, image),
+                    gram(image, weighted),
+                ),
+                "gy",
             ),
-            ("gz", "gy"),
+            "gz",
         )
         step_size = spd_solve(curvature, summed_rho)
         iterate = iterate + combine(direction, step_size)

time: 469 us -> 400 us (0.85)
  blocking collectives: 186 us -> 120 us
    psum x3, blocking collectives: 186 us -> 12.9 us  [on_device(): lax.psum((gram(residual, scaled), gram(direction, image), gram(scaled, im...]
    psum x0 -> x3, blocking collectives: none -> 107 us  [on_device(): lax.psum(lax.psum((gram(residual, scaled), gram(direction, image), gram(s...]
  transfers between devices with their start and end apart: 16 -> 16, of which waited for: 9 -> 9; matrix products, arithmetic and copies ran while one was open for 5% -> 6% of each run, Pallas kernels for 0% -> 0%
where the time goes in v1:
time: 400 us; the launch traced here: 394 us
  blocking collectives  120 us (30%)
  waiting for transfers between devices  105 us (26%)
  matrix products  68.6 us (17%)
  starting transfers between devices  39.8 us (10%)
  other arithmetic  33.6 us (8%)
  local copies, waits for them, and re-layouts  24.9 us (6%)
    psum x3, blocking collectives, on_device(): lax.psum(lax.psum((gram(residual, scaled), gram(direction, image), gram(s...  107 us
    ppermute x8, waiting for transfers between devices, extended_2(): lax.ppermute(tail, axis, [(i, (i + 1) % count) for i in range(ends)])  63.4 us
    ppermute x8, waiting for transfers between devices, extended_2(): lax.ppermute(head, axis, [((i + 1) % count, i) for i in range(ends)])  41.8 us
    dot_general x8, matrix products, combine(): lax.dot_general(weights, flat, (((0,), (0,)), ((), ())), precision=highest)  38.8 us
    ppermute x8, starting transfers between devices, extended_2(): lax.ppermute(tail, axis, [(i, (i + 1) % count) for i in range(ends)])  28.6 us
    dot_general x9, matrix products, gram(): lax.dot_general(left_flat, right_flat, (((1,), (1,)), ((), ())), precisio...  26.9 us
    unnamed x22, local copies, waits for them, and re-layouts  21.5 us
    psum x3, blocking collectives, on_device(): lax.psum((gram(residual, scaled), gram(direction, image), gram(scaled, im...  12.9 us
  transfers between devices with their start and end apart: 16, of which 9 were waited for; matrix products, arithmetic and copies ran while one was open for 6% of the time, Pallas kernels for 0%

profile of v1, /device:TPU:0, one launch (start us, length us, event | category | flops | bytes accessed | tf_op | source)
XLA Modules:
  0.0 393.8 jit_solution(5447394982308102620)
XLA Ops:
  2.5 1.3 collective-permute-start.1
  3.8 5.5 %collective-permute-start = (f32[2,1,64,256]{3,2,1,0:T(8,128)S(1)}, f32[2,1,64,256]{3,2,1,0:T(8,128)S(1)}, u32[]{:S(2)}, u32[]{:S(2)}) collective-permute-start(f32[2,1,64,256]{3,2,1,0:T(8,128)S(1)} %get-tuple-element.60), channel_id=1, source_target_pairs={{0,2},{2,4},{4,6},{6,8},{8,10},{10,12},{12,14},{1,3},{3,5},{5,7},{... | collective-permute-start | bytes 393224 | tf_op jit(solution)/shard_map/ppermute | solution.py:21
  9.3 1.5 collective-permute-done.1
  10.9 3.0 collective-permute-done
  13.9 1.3 collective-permute-start.3
  15.2 3.0 collective-permute-start.2
  22.1 1.3 collective-permute-start.4
  23.4 5.1 %collective-permute-start.5 = (f32[16,1,64,256]{3,0,2,1:T(8,128)S(1)}, f32[16,1,64,256]{3,0,2,1:T(8,128)S(1)}, u32[]{:S(2)}, u32[]{:S(2)}) collective-permute-start(f32[16,1,64,256]{3,0,2,1:T(8,128)S(1)} %get-tuple-element.44), channel_id=1, source_target_pairs={{0,2},{2,4},{4,6},{6,8},{8,10},{10,12},{12,14},{1,3},{3,5},{5,7},{... | collective-permute-start | bytes 3145736 | tf_op jit(solution)/shard_map/ppermute | solution.py:21
  28.5 3.5 fusion.74
  32.7 17.4 %collective-permute-done.4 = f32[16,1,64,256]{3,0,2,1:T(8,128)S(1)} collective-permute-done((f32[16,1,64,256]{3,0,2,1:T(8,128)S(1)}, f32[16,1,64,256]{3,0,2,1:T(8,128)S(1)}, u32[]{:S(2)}, u32[]{:S(2)}) %collective-permute-start.4) | collective-permute-done | bytes 1048608 | tf_op jit(solution)/shard_map/ppermute | solution.py:23
  50.1 22.6 %collective-permute-done.5 = f32[16,1,64,256]{3,0,2,1:T(8,128)S(1)} collective-permute-done((f32[16,1,64,256]{3,0,2,1:T(8,128)S(1)}, f32[16,1,64,256]{3,0,2,1:T(8,128)S(1)}, u32[]{:S(2)}, u32[]{:S(2)}) %collective-permute-start.5) | collective-permute-done | bytes 1048608 | tf_op jit(solution)/shard_map/ppermute | solution.py:21
  72.8 1.9 collective-permute-start.7
  74.7 1.5 collective-permute-start.6
  76.4 2.5 copy.93
  79.0 3.2 fusion.34
  82.2 3.8 convolution_bitcast_fusion.5
  86.0 2.7 fusion.86
  88.8 2.6 copy.95
  91.3 4.4 %all-reduce.15 = (f32[16,16]{0,1:T(8,128)S(1)}, f32[16,16]{0,1:T(8,128)S(1)}, f32[16,16]{1,0:T(8,128)S(1)}) all-reduce(f32[16,16]{0,1:T(8,128)S(1)} %fusion.74, f32[16,16]{0,1:T(8,128)S(1)} %convolution_bitcast_fusion.5, f32[16,16]{1,0:T(8,128)S(1)} %fusion.86), channel_id=1, replica_groups=mesh['regions'=2,'gz'=8,'gy'=2] {'gy'}, use_global_device_ids=true, to_apply=%region_4.6 | all-reduce | flops 768 | bytes 6144 | tf_op jit(solution)/shard_map/psum | solution.py:114
  95.7 36.0 %all-reduce.12 = (f32[16,16]{0,1:T(8,128)S(1)}, f32[16,16]{0,1:T(8,128)S(1)}, f32[16,16]{1,0:T(8,128)S(1)}) all-reduce(f32[16,16]{0,1:T(8,128)S(1)} %get-tuple-element.23, f32[16,16]{0,1:T(8,128)S(1)} %get-tuple-element.24, f32[16,16]{1,0:T(8,128)S(1)} %get-tuple-element.25), channel_id=1, replica_groups=mesh['regions'=2,'gz'=8,'gy'=2] {'gz'}, use_global_device_ids=true, to_apply=%region_5.7 | all-reduce | flops 768 | bytes 6144 | tf_op jit(solution)/shard_map/psum | solution.py:113
  131.8 1.5 cholesky.89
  134.7 1.2 custom-call.11
  136.5 6.3 %copy_subtract_fusion = f32[16,2,64,256]{3,0,2,1:T(8,128)S(1)} fusion(f32[16,2,64,256]{3,2,1,0:T(8,128)} %param.8, f32[2,64,256,16]{2,1,0,3:T(8,128)} %bitcast.241, f32[16,16]{1,0:T(8,128)S(1)} %fusion.124), kind=kOutput, calls=%fused_computation.85 | convolution fusion | flops 101187584 | bytes 6292480 | tf_op jit(solution)/shard_map/dot_general | solution.py:89
  143.0 1.5 cholesky.100
  147.6 4.5 %multiply_add_fusion.1 = f32[16,2,64,256]{3,0,2,1:T(8,128)S(1)} fusion(f32[16,2,64,256]{3,0,2,1:T(8,128)S(1)} %copy_subtract_fusion, f32[16,16,1,1]{0,1,3,2:T(8,128)S(1)} %convolution_bitcast_fusion.4, f32[2,64,256,16]{2,1,0,3:T(8,128)} %bitcast.236, f32[2,64,256]{2,1,0:T(8,128)S(1)} %get-tuple-element.26), kind=kOutput, calls=%fused_computation.11 | convolution fusion | flops 101711872 | bytes 6423552 | tf_op jit(solution)/shard_map/dot_general | solution.py:89
  152.3 1.3 collective-permute-start.8
  153.6 4.6 %collective-permute-start.9 = (f32[16,1,64,256]{3,0,2,1:T(8,128)S(1)}, f32[16,1,64,256]{3,0,2,1:T(8,128)S(1)}, u32[]{:S(2)}, u32[]{:S(2)}) collective-permute-start(f32[16,1,64,256]{3,0,2,1:T(8,128)S(1)} %get-tuple-element.40), channel_id=1, source_target_pairs={{0,2},{2,4},{4,6},{6,8},{8,10},{10,12},{12,14},{1,3},{3,5},{5,7},{... | collective-permute-start | bytes 3145736 | tf_op jit(solution)/shard_map/ppermute | solution.py:21
  159.0 13.8 %collective-permute-done.8 = f32[16,1,64,256]{3,0,2,1:T(8,128)S(1)} collective-permute-done((f32[16,1,64,256]{3,0,2,1:T(8,128)S(1)}, f32[16,1,64,256]{3,0,2,1:T(8,128)S(1)}, u32[]{:S(2)}, u32[]{:S(2)}) %collective-permute-start.8) | collective-permute-done | bytes 1048608 | tf_op jit(solution)/shard_map/ppermute | solution.py:23
  172.8 18.2 %collective-permute-done.9 = f32[16,1,64,256]{3,0,2,1:T(8,128)S(1)} collective-permute-done((f32[16,1,64,256]{3,0,2,1:T(8,128)S(1)}, f32[16,1,64,256]{3,0,2,1:T(8,128)S(1)}, u32[]{:S(2)}, u32[]{:S(2)}) %collective-permute-start.9) | collective-permute-done | bytes 1048608 | tf_op jit(solution)/shard_map/ppermute | solution.py:21
  191.0 1.9 collective-permute-start.11
  193.0 1.8 collective-permute-start.10
  194.8 2.8 fusion.77
  197.6 2.6 copy.97
  200.2 3.2 fusion.24
  203.4 2.9 convolution_bitcast_fusion.3
  206.3 2.8 fusion.89
  209.1 2.8 fusion.80
  211.9 2.6 copy.99
  214.4 4.4 %all-reduce.14 = (f32[16,16]{0,1:T(8,128)S(1)}, f32[16,16]{0,1:T(8,128)S(1)}, f32[16,16]{1,0:T(8,128)S(1)}, f32[16,16]{1,0:T(8,128)S(1)}) all-reduce(f32[16,16]{0,1:T(8,128)S(1)} %fusion.77, f32[16,16]{0,1:T(8,128)S(1)} %convolution_bitcast_fusion.3, f32[16,16]{1,0:T(8,128)S(1)} %fusion.89, ...), channel_id=1, replica_groups=mesh['regions'=2,'gz'=8,'gy'=2] {'gy'}, use_global_device_ids=true, to_apply=%region_10.13 | all-reduce | flops 1024 | bytes 8192 | tf_op jit(solution)/shard_map/psum | solution.py:114
  218.8 35.7 %all-reduce.11 = (f32[16,16]{0,1:T(8,128)S(1)}, f32[16,16]{0,1:T(8,128)S(1)}, f32[16,16]{1,0:T(8,128)S(1)}, f32[16,16]{1,0:T(8,128)S(1)}) all-reduce(f32[16,16]{0,1:T(8,128)S(1)} %get-tuple-element.19, f32[16,16]{0,1:T(8,128)S(1)} %get-tuple-element.20, ...), channel_id=1, replica_groups=mesh['regions'=2,'gz'=8,'gy'=2] {'gz'}, use_global_device_ids=true, to_apply=%region_11.14 | all-reduce | flops 1024 | bytes 8192 | tf_op jit(solution)/shard_map/psum | solution.py:113
  254.6 1.5 cholesky.111
  259.0 5.6 %fusion.68 = f32[16,2,64,256]{3,0,2,1:T(8,128)} fusion(f32[16,2,64,256]{3,0,2,1:T(8,128)S(1)} %copy_subtract_fusion, f32[2,64,256,16]{2,1,0,3:T(8,128)} %bitcast.240, f32[16,16]{1,0:T(8,128)S(1)} %fusion.113), kind=kOutput, calls=%fused_computation.89 | convolution fusion | flops 101187584 | bytes 6292480 | tf_op jit(solution)/shard_map/dot_general | solution.py:89
  265.0 1.5 cholesky.122
  269.6 5.2 %multiply_add_fusion = f32[16,2,64,256]{3,0,2,1:T(8,128)S(1)} fusion(f32[16,2,64,256]{3,0,2,1:T(8,128)} %fusion.68, f32[16,16,1,1]{0,1,3,2:T(8,128)S(1)} %convolution_bitcast_fusion.2, f32[2,64,256,16]{2,1,0,3:T(8,128)} %bitcast.234, f32[2,64,256]{2,1,0:T(8,128)S(1)} %get-tuple-element.26), kind=kOutput, calls=%fused_computation.6 | convolution fusion | flops 101711872 | bytes 6423552 | tf_op jit(solution)/shard_map/dot_general | solution.py:89
  275.0 1.4 collective-permute-start.12
  276.4 4.6 %collective-permute-start.13 = (f32[16,1,64,256]{3,0,2,1:T(8,128)S(1)}, f32[16,1,64,256]{3,0,2,1:T(8,128)S(1)}, u32[]{:S(2)}, u32[]{:S(2)}) collective-permute-start(f32[16,1,64,256]{3,0,2,1:T(8,128)S(1)} %get-tuple-element.36), channel_id=1, source_target_pairs={{0,2},{2,4},{4,6},{6,8},{8,10},{10,12},{12,14},{1,3},{3,5},{5,7},{... | collective-permute-start | bytes 3145736 | tf_op jit(solution)/shard_map/ppermute | solution.py:21
  281.0 4.2 %fusion.52 = f32[16,2,64,256]{3,0,2,1:T(8,128)} fusion(f32[2,64,256,16]{2,1,0,3:T(8,128)S(1)} %bitcast.235, f32[16,16]{1,0:T(8,128)S(1)} %fusion.113), kind=kOutput, calls=%fused_computation.79 | convolution fusion | flops 100663296 | bytes 4195328 | tf_op jit(solution)/shard_map/dot_general | solution.py:89
  286.0 9.0 %collective-permute-done.12 = f32[16,1,64,256]{3,0,2,1:T(8,128)S(1)} collective-permute-done((f32[16,1,64,256]{3,0,2,1:T(8,128)S(1)}, f32[16,1,64,256]{3,0,2,1:T(8,128)S(1)}, u32[]{:S(2)}, u32[]{:S(2)}) %collective-permute-start.12) | collective-permute-done | bytes 1048608 | tf_op jit(solution)/shard_map/ppermute | solution.py:23
  295.0 18.8 %collective-permute-done.13 = f32[16,1,64,256]{3,0,2,1:T(8,128)S(1)} collective-permute-done((f32[16,1,64,256]{3,0,2,1:T(8,128)S(1)}, f32[16,1,64,256]{3,0,2,1:T(8,128)S(1)}, u32[]{:S(2)}, u32[]{:S(2)}) %collective-permute-start.13) | collective-permute-done | bytes 1048608 | tf_op jit(solution)/shard_map/ppermute | solution.py:21
  313.8 1.9 collective-permute-start.15
  315.7 1.3 collective-permute-start.14
  317.0 2.8 fusion.83
  319.8 2.6 copy.101
  322.4 3.2 fusion.14
  325.6 1.3 copy-done.4
  326.9 2.9 convolution_bitcast_fusion.1
  329.8 4.2 %all-reduce.13 = (f32[16,16]{1,0:T(8,128)S(1)}, f32[16,16]{0,1:T(8,128)S(1)}) all-reduce(f32[16,16]{1,0:T(8,128)S(1)} %fusion.83, f32[16,16]{0,1:T(8,128)S(1)} %convolution_bitcast_fusion.1), channel_id=1, replica_groups=mesh['regions'=2,'gz'=8,'gy'=2] {'gy'}, use_global_device_ids=true, to_apply=%region_18.21 | all-reduce | flops 512 | bytes 4096 | tf_op jit(solution)/shard_map/psum | solution.py:114
  334.0 35.5 %all-reduce.10 = (f32[16,16]{1,0:T(8,128)S(1)}, f32[16,16]{0,1:T(8,128)S(1)}) all-reduce(f32[16,16]{1,0:T(8,128)S(1)} %get-tuple-element.17, f32[16,16]{0,1:T(8,128)S(1)} %get-tuple-element.18), channel_id=1, replica_groups=mesh['regions'=2,'gz'=8,'gy'=2] {'gz'}, use_global_device_ids=true, to_apply=%region_19.22 | all-reduce | flops 512 | bytes 4096 | tf_op jit(solution)/shard_map/psum | solution.py:113
  369.6 1.5 cholesky.133
  374.0 4.5 %fusion.42 = f32[16,2,64,256]{3,0,2,1:T(8,128)S(1)} fusion(f32[16,16,1,1]{0,1,3,2:T(8,128)S(1)} %convolution_bitcast_fusion, f32[2,64,256,16]{2,1,0,3:T(8,128)} %bitcast.239), kind=kOutput, calls=%fused_computation.68 | convolution fusion | flops 100663296 | bytes 4195328 | tf_op jit(solution)/shard_map/dot_general | solution.py:89
  378.6 5.7 %fusion.49 = f32[16,2,64,256]{3,0,2,1:T(8,128)S(1)} fusion(f32[16,2,64,256]{3,0,2,1:T(8,128)S(1)} %fusion.42, f32[16,2,64,256]{3,0,2,1:T(8,128)S(1)} %copy-done.6, f32[16,2,64,256]{3,2,1,0:T(8,128)} %param.7, f32[2,64,256,16]{2,1,0,3:T(8,128)S(1)} %bitcast.237, f32[16,16]{1,0:T(8,128)S(1)} %fusion.124), kind=kOutput, calls=%fused_computation.76 | convolution fusion | flops 102236160 | bytes 10486784 | tf_op jit(solution)/shard_map/dot_general | solution.py:89
  384.3 2.5 copy.64
  388.0 2.9 fusion.71
  390.9 2.5 copy.65
  (88 shorter events, 24.8 us)
Async XLA Ops:
  2.5 8.4 %collective-permute-start.1 = (f32[2,1,64,256]{3,2,1,0:T(8,128)S(1)}, f32[2,1,64,256]{3,2,1,0:T(8,128)S(1)}, u32[]{:S(2)}, u32[]{:S(2)}) collective-permute-start(f32[2,1,64,256]{3,2,1,0:T(8,128)S(1)} %get-tuple-element.61), channel_id=1, source_target_pairs={{2,0},{4,2},{6,4},{8,6},{10,8},{12,10},{14,12},{3,1},{5,3},{7,5},{... | collective-permute-start | bytes 393224 | tf_op jit(solution)/shard_map/ppermute | solution.py:23
  3.8 10.0 %collective-permute-start = (f32[2,1,64,256]{3,2,1,0:T(8,128)S(1)}, f32[2,1,64,256]{3,2,1,0:T(8,128)S(1)}, u32[]{:S(2)}, u32[]{:S(2)}) collective-permute-start(f32[2,1,64,256]{3,2,1,0:T(8,128)S(1)} %get-tuple-element.60), channel_id=1, source_target_pairs={{0,2},{2,4},{4,6},{6,8},{8,10},{10,12},{12,14},{1,3},{3,5},{5,7},{... | collective-permute-start | bytes 393224 | tf_op jit(solution)/shard_map/ppermute | solution.py:21
  13.9 4.3 %collective-permute-start.3 = (f32[2,4,1,256]{3,2,1,0:T(1,128)S(1)}, f32[2,4,1,256]{3,2,1,0:T(1,128)S(1)}, u32[]{:S(2)}, u32[]{:S(2)}) collective-permute-start(f32[2,4,1,256]{3,2,1,0:T(1,128)S(1)} %get-tuple-element.55), channel_id=1, source_target_pairs={{1,0},{3,2},{5,4},{7,6},{9,8},{11,10},{13,12},{15,14},{17,16},{19,... | collective-permute-start | bytes 24584 | tf_op jit(solution)/shard_map/ppermute | solution.py:23
  15.2 3.8 collective-permute-start.2
  19.1 1.6 copy-start
  22.1 28.1 %collective-permute-start.4 = (f32[16,1,64,256]{3,0,2,1:T(8,128)S(1)}, f32[16,1,64,256]{3,0,2,1:T(8,128)S(1)}, u32[]{:S(2)}, u32[]{:S(2)}) collective-permute-start(f32[16,1,64,256]{3,0,2,1:T(8,128)S(1)} %get-tuple-element.45), channel_id=1, source_target_pairs={{2,0},{4,2},{6,4},{8,6},{10,8},{12,10},{14,12},{3,1},{5,3},{7,5},{... | collective-permute-start | bytes 3145736 | tf_op jit(solution)/shard_map/ppermute | solution.py:23
  23.4 49.4 %collective-permute-start.5 = (f32[16,1,64,256]{3,0,2,1:T(8,128)S(1)}, f32[16,1,64,256]{3,0,2,1:T(8,128)S(1)}, u32[]{:S(2)}, u32[]{:S(2)}) collective-permute-start(f32[16,1,64,256]{3,0,2,1:T(8,128)S(1)} %get-tuple-element.44), channel_id=1, source_target_pairs={{0,2},{2,4},{4,6},{6,8},{8,10},{10,12},{12,14},{1,3},{3,5},{5,7},{... | collective-permute-start | bytes 3145736 | tf_op jit(solution)/shard_map/ppermute | solution.py:21
  72.8 6.2 %collective-permute-start.7 = (f32[16,4,1,256]{3,0,2,1:T(8,128)S(1)}, f32[16,4,1,256]{3,0,2,1:T(8,128)S(1)}, u32[]{:S(2)}, u32[]{:S(2)}) collective-permute-start(f32[16,4,1,256]{3,0,2,1:T(8,128)S(1)} %get-tuple-element.33), channel_id=1, source_target_pairs={{0,1},{2,3},{4,5},{6,7},{8,9},{10,11},{12,13},{14,15},{16,17},{18,... | collective-permute-start | bytes 196616 | tf_op jit(solution)/shard_map/ppermute | solution.py:21
  74.7 4.3 %collective-permute-start.6 = (f32[16,4,1,256]{3,0,2,1:T(8,128)S(1)}, f32[16,4,1,256]{3,0,2,1:T(8,128)S(1)}, u32[]{:S(2)}, u32[]{:S(2)}) collective-permute-start(f32[16,4,1,256]{3,0,2,1:T(8,128)S(1)} %get-tuple-element.32), channel_id=1, source_target_pairs={{1,0},{3,2},{5,4},{7,6},{9,8},{11,10},{13,12},{15,14},{17,16},{19,... | collective-permute-start | bytes 196616 | tf_op jit(solution)/shard_map/ppermute | solution.py:23
  152.3 20.5 %collective-permute-start.8 = (f32[16,1,64,256]{3,0,2,1:T(8,128)S(1)}, f32[16,1,64,256]{3,0,2,1:T(8,128)S(1)}, u32[]{:S(2)}, u32[]{:S(2)}) collective-permute-start(f32[16,1,64,256]{3,0,2,1:T(8,128)S(1)} %get-tuple-element.41), channel_id=1, source_target_pairs={{2,0},{4,2},{6,4},{8,6},{10,8},{12,10},{14,12},{3,1},{5,3},{7,5},{... | collective-permute-start | bytes 3145736 | tf_op jit(solution)/shard_map/ppermute | solution.py:23
  153.6 37.4 %collective-permute-start.9 = (f32[16,1,64,256]{3,0,2,1:T(8,128)S(1)}, f32[16,1,64,256]{3,0,2,1:T(8,128)S(1)}, u32[]{:S(2)}, u32[]{:S(2)}) collective-permute-start(f32[16,1,64,256]{3,0,2,1:T(8,128)S(1)} %get-tuple-element.40), channel_id=1, source_target_pairs={{0,2},{2,4},{4,6},{6,8},{8,10},{10,12},{12,14},{1,3},{3,5},{5,7},{... | collective-permute-start | bytes 3145736 | tf_op jit(solution)/shard_map/ppermute | solution.py:21
  191.0 9.1 %collective-permute-start.11 = (f32[16,4,1,256]{3,0,2,1:T(8,128)S(1)}, f32[16,4,1,256]{3,0,2,1:T(8,128)S(1)}, u32[]{:S(2)}, u32[]{:S(2)}) collective-permute-start(f32[16,4,1,256]{3,0,2,1:T(8,128)S(1)} %get-tuple-element.31), channel_id=1, source_target_pairs={{0,1},{2,3},{4,5},{6,7},{8,9},{10,11},{12,13},{14,15},{16,17},{18,... | collective-permute-start | bytes 196616 | tf_op jit(solution)/shard_map/ppermute | solution.py:21
  193.0 7.2 %collective-permute-start.10 = (f32[16,4,1,256]{3,0,2,1:T(8,128)S(1)}, f32[16,4,1,256]{3,0,2,1:T(8,128)S(1)}, u32[]{:S(2)}, u32[]{:S(2)}) collective-permute-start(f32[16,4,1,256]{3,0,2,1:T(8,128)S(1)} %get-tuple-element.30), channel_id=1, source_target_pairs={{1,0},{3,2},{5,4},{7,6},{9,8},{11,10},{13,12},{15,14},{17,16},{19,... | collective-permute-start | bytes 196616 | tf_op jit(solution)/shard_map/ppermute | solution.py:23
  274.8 6.2 %copy-start.2 = (f32[2,8,128,256]{3,2,1,0:T(8,128)S(1)}, f32[2,8,128,256]{3,2,1,0:T(8,128)}, u32[]{:S(2)}) copy-start(f32[2,8,128,256]{3,2,1,0:T(8,128)} %copy.97) | copy-start | bytes 6291460
  275.0 20.0 %collective-permute-start.12 = (f32[16,1,64,256]{3,0,2,1:T(8,128)S(1)}, f32[16,1,64,256]{3,0,2,1:T(8,128)S(1)}, u32[]{:S(2)}, u32[]{:S(2)}) collective-permute-start(f32[16,1,64,256]{3,0,2,1:T(8,128)S(1)} %get-tuple-element.37), channel_id=1, source_target_pairs={{2,0},{4,2},{6,4},{8,6},{10,8},{12,10},{14,12},{3,1},{5,3},{7,5},{... | collective-permute-start | bytes 3145736 | tf_op jit(solution)/shard_map/ppermute | solution.py:23
  276.4 37.4 %collective-permute-start.13 = (f32[16,1,64,256]{3,0,2,1:T(8,128)S(1)}, f32[16,1,64,256]{3,0,2,1:T(8,128)S(1)}, u32[]{:S(2)}, u32[]{:S(2)}) collective-permute-start(f32[16,1,64,256]{3,0,2,1:T(8,128)S(1)} %get-tuple-element.36), channel_id=1, source_target_pairs={{0,2},{2,4},{4,6},{6,8},{8,10},{10,12},{12,14},{1,3},{3,5},{5,7},{... | collective-permute-start | bytes 3145736 | tf_op jit(solution)/shard_map/ppermute | solution.py:21
  286.0 31.0 %copy-start.1 = (f32[16,2,64,256]{3,0,2,1:T(8,128)S(1)}, f32[16,2,64,256]{3,0,2,1:T(8,128)}, u32[]{:S(2)}) copy-start(f32[16,2,64,256]{3,0,2,1:T(8,128)} %fusion.68) | copy-start | bytes 6291460
  313.8 8.6 %collective-permute-start.15 = (f32[16,4,1,256]{3,0,2,1:T(8,128)S(1)}, f32[16,4,1,256]{3,0,2,1:T(8,128)S(1)}, u32[]{:S(2)}, u32[]{:S(2)}) collective-permute-start(f32[16,4,1,256]{3,0,2,1:T(8,128)S(1)} %get-tuple-element.29), channel_id=1, source_target_pairs={{0,1},{2,3},{4,5},{6,7},{8,9},{10,11},{12,13},{14,15},{16,17},{18,... | collective-permute-start | bytes 196616 | tf_op jit(solution)/shard_map/ppermute | solution.py:21
  315.7 6.6 %collective-permute-start.14 = (f32[16,4,1,256]{3,0,2,1:T(8,128)S(1)}, f32[16,4,1,256]{3,0,2,1:T(8,128)S(1)}, u32[]{:S(2)}, u32[]{:S(2)}) collective-permute-start(f32[16,4,1,256]{3,0,2,1:T(8,128)S(1)} %get-tuple-element.28), channel_id=1, source_target_pairs={{1,0},{3,2},{5,4},{7,6},{9,8},{11,10},{13,12},{15,14},{17,16},{19,... | collective-permute-start | bytes 196616 | tf_op jit(solution)/shard_map/ppermute | solution.py:23
  325.6 1.3 copy-start.4
  374.0 4.6 %copy-start.3 = (f32[2,8,128,256]{3,2,1,0:T(8,128)S(1)}, f32[2,8,128,256]{3,2,1,0:T(8,128)}, u32[]{:S(2)}) copy-start(f32[2,8,128,256]{3,2,1,0:T(8,128)} %copy.93) | copy-start | bytes 6291460
  374.0 4.6 %copy-start.6 = (f32[16,2,64,256]{3,0,2,1:T(8,128)S(1)}, f32[16,2,64,256]{3,0,2,1:T(8,128)}, u32[]{:S(2)}) copy-start(f32[16,2,64,256]{3,0,2,1:T(8,128)} %fusion.52) | copy-start | bytes 6291460
  384.3 2.5 copy-start.5
